TPU v7x, 256 devices: a whole 4x4x8 slice. The times are simulated.
256 devices in a mesh: view: 16 (over y, x), scene: 16 (over z, core).
Axes of the slice: x: 4, y: 4, z: 8, core: 2. Of those that a mesh axis runs over, the one named last changes fastest.
Arguments:
- params: float32 [14, 262144], P(None, 'scene'), may hold values from -3 to 3
- pixel_basis: float32 [512, 13, 256], P('view'), may hold values from -6 to 6
- tile_blocks: int32 [512, 16, 2], P('view', 'scene'), may hold values from 0 to 127
- depth_rank: int32 [512, 32], P('view'), may hold values from 0 to 31, each once within a row
- target: float32 [512, 256], P('view'), may hold values from -0.3 to 0.3
Outputs:
- step: float32 [14, 262144], P(None, 'scene')
- residual: float32 [512, 256], P('view')
Inputs may be any that keep to these rules, and one draw needn't show every extreme that they name: `tile_blocks`: index of a block among the 128 blocks held by the owner named by the second dimension; a tile may list a block more than once. `depth_rank`: each row is a permutation of the 32 slots; a lower rank lies in front.
All inputs are finite; a program needn't handle non-finite values.
Results may differ from a plain program's by a relative error of at most 0.0003.
Values sent between devices are 32-bit elements; how exact they have to be, the bound alone decides.
A program may use at most 128 MiB of HBM per device.

v0:
```python
import jax
import jax.numpy as jnp
from jax import lax
from jax.sharding import PartitionSpec as P

BLOCK_SIZE = 128
ITERS = 3
alpha_max = 0.004
damping = 0.1
ridge_term = 0.0001
highest = lax.Precision.HIGHEST


def local(params, pixel_basis, tile_blocks, depth_rank, target):
    param_count = params.shape[0]
    tile_count = pixel_basis.shape[0]
    owned_slots = tile_blocks.shape[2]
    block_width = BLOCK_SIZE
    blocks = params.shape[1] // block_width
    param_blocks = params.reshape(param_count, blocks, block_width)
    pair_ids = tile_blocks.reshape(tile_count * owned_slots)
    onehot = (pair_ids[:, None] == jnp.arange(blocks, dtype=jnp.int32)[None, :]).astype(jnp.float32)
    position = lax.broadcasted_iota(jnp.int32, (block_width, block_width), 0)
    later_index = lax.broadcasted_iota(jnp.int32, (block_width, block_width), 1)
    strict = (position < later_index).astype(jnp.float32)
    pieces = jnp.take(param_blocks, pair_ids, axis=1).reshape(
        param_count, tile_count, owned_slots, block_width
    )
    logits = jnp.einsum("tcq,ctjg->tjqg", pixel_basis, pieces[: param_count - 1], precision=highest)
    opacity = alpha_max * jax.nn.sigmoid(logits)
    log_keep = jnp.log1p(-opacity)
    inner_log = jnp.einsum("tjqg,gh->tjqh", log_keep, strict, precision=highest)
    colour, opacity, log_keep, inner_log = (pieces[param_count - 1], opacity, log_keep, inner_log)
    block_log = jnp.sum(log_keep, axis=3)
    all_logs = lax.all_gather(block_log, "scene", axis=1, tiled=True)
    own_rank = lax.dynamic_slice_in_dim(
        depth_rank, lax.axis_index("scene") * owned_slots, owned_slots, 1
    )
    earlier = (depth_rank[:, None, :] < own_rank[:, :, None]).astype(jnp.float32)
    front_log = jnp.einsum("tjl,tlq->tjq", earlier, all_logs, precision=highest)
    weight_now = jnp.exp(front_log[:, :, :, None] + inner_log) * opacity
    slope_now = weight_now * colour[:, :, None, :] * (1.0 - opacity / alpha_max)
    weight = weight_now
    slopes = slope_now
    render_part = jnp.sum(weight * colour[:, :, None, :], axis=(1, 3))
    render = lax.psum(render_part, "scene")
    residual = render - target

    def to_blocks(feature, colour_term):
        stacked = jnp.concatenate([feature, colour_term[None]], axis=0)
        stacked = stacked.reshape(param_count, tile_count * owned_slots, block_width)
        return jnp.einsum("cpg,pb->cbg", stacked, onehot, precision=highest)

    def transpose_apply(weight_now, slope_now, pixel_vec):
        spread = pixel_vec[:, None, :, None]
        feature = jnp.einsum("tcq,tjqg->ctjg", pixel_basis, slope_now * spread, precision=highest)
        colour_term = jnp.sum(weight_now * spread, axis=2)
        return to_blocks(feature, colour_term)

    grad_part = transpose_apply(weight, slopes, residual)
    diag_feature = jnp.einsum(
        "tcq,tjqg->ctjg", pixel_basis * pixel_basis, slopes * slopes, precision=highest
    )
    diag_part = to_blocks(diag_feature, jnp.sum(weight * weight, axis=2))
    gradient, curv_diag = lax.psum((grad_part, diag_part), "view")

    def inner_sum(first_vec, second_vec):
        local_sum = jnp.sum(first_vec * second_vec)
        return lax.psum(local_sum, "scene")

    precondition = (1.0 + damping) * curv_diag + ridge_term
    solution = jnp.zeros_like(gradient)
    remainder = -gradient
    scaled = remainder / precondition
    direction = scaled
    rho_now = inner_sum(remainder, scaled)
    for iteration in range(ITERS):
        full_dir = direction
        forward_pieces = jnp.take(full_dir, pair_ids, axis=1).reshape(
            param_count, tile_count, owned_slots, block_width
        )
        projected = jnp.einsum(
            "tcq,ctjg->tjqg", pixel_basis, forward_pieces[: param_count - 1], precision=highest
        )
        partial_value = jnp.sum(
            slopes * projected + weight * forward_pieces[param_count - 1][:, :, None, :],
            axis=(1, 3),
        )
        curvature_pixel_vec = lax.psum(partial_value, "scene")
        curvature_partial_value = transpose_apply(weight, slopes, curvature_pixel_vec)
        reduced = lax.psum(curvature_partial_value, "view")
        image_dir = reduced + (damping * curv_diag + ridge_term) * direction
        step_size = rho_now / inner_sum(direction, image_dir)
        solution = solution + step_size * direction
        if iteration + 1 < ITERS:
            remainder = remainder - step_size * image_dir
            scaled = remainder / precondition
            rho_next = inner_sum(remainder, scaled)
            direction = scaled + rho_next / rho_now * direction
            rho_now = rho_next
    return (solution.reshape(param_count, blocks * block_width), residual)


def solution(mesh):
    in_specs = (
        P(None, "scene"),
        P("view", None, None),
        P("view", "scene", None),
        P("view", None),
        P("view", None),
    )
    out_specs = (P(None, "scene"), P("view", None))
    return jax.shard_map(local, mesh=mesh, in_specs=in_specs, out_specs=out_specs, check_vma=False)
```

profile of v0, /device:TPU:1, one launch (start us, length us, event | category | flops | bytes accessed | tf_op | source)
XLA Modules:
  0.0 938.0 jit_solution(4138145236380710642)
XLA Ops:
  11.0 14.0 %fusion.19 = (f32[32,2,256]{2,1,0:T(2,128)S(1)}, f32[32,2,128,256]{3,2,1,0:T(8,128)}) fusion(f32[13,32,2,128]{3,0,2,1:T(8,128)S(1)} %bitcast.140, f32[32,13,256,1]{2,0,1,3:T(8,128)} %bitcast.120), kind=kOutput, calls=%fused_computation.35 | convolution fusion | flops 339722240 | bytes 9306112 | tf_op jit(solution)/shard_map/tcq,ctjg->tjqg/dot_general | solution.py:29
  26.1 42.5 %all-gather.2.cloned.1.call-done = f32[32,32,256]{2,0,1:T(8,128)} async-done(((f32[32,2,256]{2,0,1:T(8,128)}), f32[32,32,256]{2,0,1:T(8,128)}) %all-gather.2.cloned.1.call-update) | async-done | bytes 1048592 | tf_op jit(solution)/shard_map/all_gather | solution.py:35
  70.8 18.9 %bitcast_multiply_fusion.3 = (f32[32,2,256,128]{2,3,1,0:T(8,128)}, f32[32,256]{1,0:T(8,128)S(1)}, f32[32,2,256,128]{2,3,1,0:T(8,128)}) fusion(f32[32,2,128,256]{3,2,1,0:T(8,128)} %get-tuple-element.14, f32[32,2,128]{2,1,0:T(2,128)S(1)} %bitcast.146, f32[32,2,256]{2,1,0:T(2,128)S(1)} %fusion.27), kind=kOutput, calls=%fused_computation.13 | convolution fusion | flops 3240108032 | bytes 25296896 | tf_op jit(solution)/shard_map/tjqg,gh->tjqh/dot_general | solution.py:32
  89.8 43.5 %psum.105 = f32[32,256]{1,0:T(8,128)S(1)} all-reduce(f32[32,256]{1,0:T(8,128)S(1)} %get-tuple-element.12), channel_id=1, replica_groups=mesh['view'=16,'scene'=16] {'scene'}, use_global_device_ids=true, to_apply=%region_2.4 | all-reduce | flops 8192 | bytes 65536 | tf_op jit(solution)/shard_map/psum | solution.py:46
  133.3 10.4 %fusion.15 = f32[32,2,128,13]{2,3,1,0:T(8,128)S(1)} fusion(f32[32,2,256,128]{2,3,1,0:T(8,128)} %get-tuple-element.11, f32[32,256]{1,0:T(8,128)S(1)} %sub.13, f32[32,13,256,1]{2,0,1,3:T(8,128)S(1)} %bitcast.121), kind=kOutput, calls=%fused_computation.30 | convolution fusion | flops 329252864 | bytes 9273344 | tf_op jit(solution)/shard_map/tcq,tjqg->ctjg/dot_general | solution.py:56
  146.3 7.5 fusion.13
  157.1 101.0 %all-reduce.13.cloned.1.call-done = (f32[14,128,128]{2,1,0:T(8,128)}, f32[14,128,128]{2,1,0:T(8,128)}) async-done(((f32[14,128,128]{2,1,0:T(8,128)}, f32[14,128,128]{2,1,0:T(8,128)}), (f32[14,128,128]{2,1,0:T(8,128)}, f32[14,128,128]{2,1,0:T(8,128)})) %all-reduce.13.cloned.1.call-update) | async-done | bytes 1835024 | tf_op jit(solution)/shard_map/psum | solution.py:65
  261.2 12.3 %fusion.5 = f32[32,256]{1,0:T(8,128)S(1)} fusion(f32[32,2,256,128]{2,3,1,0:T(8,128)} %get-tuple-element.11, f32[32,2,256,128]{2,3,1,0:T(8,128)} %get-tuple-element.15, f32[32,2,128]{2,1,0:T(2,128)S(1)} %bitcast.147, f32[13,32,2,128]{3,0,2,1:T(8,128)S(1)} %bitcast.131, f32[32,13,256,1]{2,0,1,3:T(8,128)S(1)} %bitcast.122), kind=kOutput, calls=%fused_computation.12 | convolution fusion | flops 335536128 | bytes 17694720 | tf_op jit(solution)/shard_map/tcq,ctjg->tjqg/dot_general | solution.py:82
  273.5 45.5 %psum.109 = f32[32,256]{1,0:T(8,128)S(1)} all-reduce(f32[32,256]{1,0:T(8,128)S(1)} %fusion.5), channel_id=1, replica_groups=mesh['view'=16,'scene'=16] {'scene'}, use_global_device_ids=true, to_apply=%region_10.12 | all-reduce | flops 8192 | bytes 65536 | tf_op jit(solution)/shard_map/psum | solution.py:89
  318.9 10.0 %fusion.11 = f32[32,2,128,13]{2,3,1,0:T(8,128)S(1)} fusion(f32[32,2,256,128]{2,3,1,0:T(8,128)} %get-tuple-element.11, f32[32,256]{1,0:T(8,128)S(1)} %psum.109, f32[32,13,256,1]{2,0,1,3:T(8,128)S(1)} %bitcast.123), kind=kOutput, calls=%fused_computation.24 | convolution fusion | flops 329252864 | bytes 9273344 | tf_op jit(solution)/shard_map/tcq,tjqg->ctjg/dot_general | solution.py:56
  335.2 96.4 %all-reduce.7.cloned.1.call-done = f32[14,128,128]{2,1,0:T(8,128)} async-done(((f32[14,128,128]{2,1,0:T(8,128)}), f32[14,128,128]{2,1,0:T(8,128)}) %all-reduce.7.cloned.1.call-update) | async-done | bytes 917520 | tf_op jit(solution)/shard_map/psum | solution.py:91
  433.9 26.2 %all-reduce = (f32[]{:T(128)}, f32[]{:T(128)}) all-reduce(f32[]{:T(128)} %get-tuple-element.6, f32[]{:T(128)} %get-tuple-element.5), channel_id=1, replica_groups=mesh['view'=16,'scene'=16] {'scene'}, use_global_device_ids=true, to_apply=%region_8.10 | all-reduce | flops 2 | bytes 16 | tf_op jit(solution)/shard_map/psum | solution.py:69
  463.7 25.1 %psum.112 = f32[]{:T(128)} all-reduce(f32[]{:T(128)} %multiply_reduce_fusion.9), channel_id=1, replica_groups=mesh['view'=16,'scene'=16] {'scene'}, use_global_device_ids=true, to_apply=%region_16.18 | all-reduce | flops 1 | bytes 8 | tf_op jit(solution)/shard_map/psum | solution.py:69
  497.1 12.1 %fusion.3 = f32[32,256]{1,0:T(8,128)S(1)} fusion(f32[32,2,256,128]{2,3,1,0:T(8,128)} %get-tuple-element.11, f32[32,2,256,128]{2,3,1,0:T(8,128)} %get-tuple-element.15, f32[32,2,128]{2,1,0:T(2,128)S(1)} %bitcast.148, f32[13,32,2,128]{3,0,2,1:T(8,128)S(1)} %bitcast.132, f32[32,13,256,1]{2,0,1,3:T(8,128)S(1)} %bitcast.124), kind=kOutput, calls=%fused_computation.9 | convolution fusion | flops 335536128 | bytes 17694720 | tf_op jit(solution)/shard_map/tcq,ctjg->tjqg/dot_general | solution.py:82
  509.2 42.8 %psum.113 = f32[32,256]{1,0:T(8,128)S(1)} all-reduce(f32[32,256]{1,0:T(8,128)S(1)} %fusion.3), channel_id=1, replica_groups=mesh['view'=16,'scene'=16] {'scene'}, use_global_device_ids=true, to_apply=%region_18.20 | all-reduce | flops 8192 | bytes 65536 | tf_op jit(solution)/shard_map/psum | solution.py:89
  552.0 9.8 %fusion.9 = f32[32,2,128,13]{2,3,1,0:T(8,128)S(1)} fusion(f32[32,2,256,128]{2,3,1,0:T(8,128)} %get-tuple-element.11, f32[32,256]{1,0:T(8,128)S(1)} %psum.113, f32[32,13,256,1]{2,0,1,3:T(8,128)S(1)} %bitcast.125), kind=kOutput, calls=%fused_computation.21 | convolution fusion | flops 329252864 | bytes 9273344 | tf_op jit(solution)/shard_map/tcq,tjqg->ctjg/dot_general | solution.py:56
  568.2 95.9 %all-reduce.9.cloned.1.call-done = f32[14,128,128]{2,1,0:T(8,128)} async-done(((f32[14,128,128]{2,1,0:T(8,128)}), f32[14,128,128]{2,1,0:T(8,128)}) %all-reduce.9.cloned.1.call-update) | async-done | bytes 917520 | tf_op jit(solution)/shard_map/psum | solution.py:91
  666.2 26.2 %psum.115 = f32[]{:T(128)} all-reduce(f32[]{:T(128)} %multiply_reduce_fusion.8), channel_id=1, replica_groups=mesh['view'=16,'scene'=16] {'scene'}, use_global_device_ids=true, to_apply=%region_22.24 | all-reduce | flops 1 | bytes 8 | tf_op jit(solution)/shard_map/psum | solution.py:69
  696.2 25.2 %psum.116 = f32[]{:T(128)} all-reduce(f32[]{:T(128)} %multiply_reduce_fusion.7), channel_id=1, replica_groups=mesh['view'=16,'scene'=16] {'scene'}, use_global_device_ids=true, to_apply=%region_24.26 | all-reduce | flops 1 | bytes 8 | tf_op jit(solution)/shard_map/psum | solution.py:69
  731.0 12.1 %fusion.1 = f32[32,256]{1,0:T(8,128)S(1)} fusion(f32[32,2,256,128]{2,3,1,0:T(8,128)} %get-tuple-element.11, f32[32,2,256,128]{2,3,1,0:T(8,128)} %get-tuple-element.15, f32[32,2,128]{2,1,0:T(2,128)S(1)} %bitcast.149, f32[13,32,2,128]{3,0,2,1:T(8,128)S(1)} %bitcast.130, f32[32,13,256,1]{2,0,1,3:T(8,128)S(1)} %bitcast.126), kind=kOutput, calls=%fused_computation.6 | convolution fusion | flops 335536128 | bytes 17694720 | tf_op jit(solution)/shard_map/tcq,ctjg->tjqg/dot_general | solution.py:82
  743.1 42.8 %psum.117 = f32[32,256]{1,0:T(8,128)S(1)} all-reduce(f32[32,256]{1,0:T(8,128)S(1)} %fusion.1), channel_id=1, replica_groups=mesh['view'=16,'scene'=16] {'scene'}, use_global_device_ids=true, to_apply=%region_26.28 | all-reduce | flops 8192 | bytes 65536 | tf_op jit(solution)/shard_map/psum | solution.py:89
  785.9 9.8 %fusion.7 = f32[32,2,128,13]{2,3,1,0:T(8,128)S(1)} fusion(f32[32,2,256,128]{2,3,1,0:T(8,128)} %get-tuple-element.11, f32[32,256]{1,0:T(8,128)S(1)} %psum.117, f32[32,13,256,1]{2,0,1,3:T(8,128)S(1)} %bitcast.127), kind=kOutput, calls=%fused_computation.18 | convolution fusion | flops 329252864 | bytes 9273344 | tf_op jit(solution)/shard_map/tcq,tjqg->ctjg/dot_general | solution.py:56
  802.1 96.0 %all-reduce.11.cloned.1.call-done = f32[14,128,128]{2,1,0:T(8,128)} async-done(((f32[14,128,128]{2,1,0:T(8,128)}), f32[14,128,128]{2,1,0:T(8,128)}) %all-reduce.11.cloned.1.call-update) | async-done | bytes 917520 | tf_op jit(solution)/shard_map/psum | solution.py:91
  900.4 26.2 %psum.119 = f32[]{:T(128)} all-reduce(f32[]{:T(128)} %multiply_reduce_fusion.6), channel_id=1, replica_groups=mesh['view'=16,'scene'=16] {'scene'}, use_global_device_ids=true, to_apply=%region_30.32 | all-reduce | flops 1 | bytes 8 | tf_op jit(solution)/shard_map/psum | solution.py:69
  (84 shorter events, 64.5 us)
Async XLA Ops:
  7.2 61.4 %all-gather.2.cloned.1.call-start = ((), (), s32[]{:S(2)}) async-start(), calls=%async_computation | async-start | bytes 1114112 | tf_op jit(solution)/shard_map/all_gather | solution.py:35
  11.0 15.0 %copy-start.6 = (s32[32,32]{1,0:T(8,128)S(1)}, s32[32,32]{1,0:T(8,128)}, u32[]{:S(2)}) copy-start(s32[32,32]{1,0:T(8,128)} %param.10) | copy-start | bytes 12292
  11.0 15.1 %copy-start.3 = (f32[32,13,256]{2,0,1:T(8,128)S(1)}, f32[32,13,256]{2,0,1:T(8,128)}, u32[]{:S(2)}) copy-start(f32[32,13,256]{2,0,1:T(8,128)} %param.8) | copy-start | bytes 1277956
  25.7 232.5 %all-reduce.13.cloned.1.call-start = ((), (), s32[]{:S(2)}) async-start(), calls=%async_computation.4 | async-start | bytes 3670016 | tf_op jit(solution)/shard_map/psum | solution.py:65
  70.8 62.5 %copy-start.7 = (f32[32,256]{1,0:T(8,128)S(1)}, f32[32,256]{1,0:T(8,128)}, u32[]{:S(2)}) copy-start(f32[32,256]{1,0:T(8,128)} %param.11) | copy-start | bytes 98308
  133.3 10.6 %copy-start = (f32[32,2,256,128]{2,3,1,0:T(8,128)S(1)}, f32[32,2,256,128]{2,3,1,0:T(8,128)}, u32[]{:S(2)}) copy-start(f32[32,2,256,128]{2,3,1,0:T(8,128)} %get-tuple-element.15) | copy-start | bytes 25165828
  133.3 12.9 %copy-start.5 = (f32[32,256]{1,0:T(8,128)}, f32[32,256]{1,0:T(8,128)S(1)}, u32[]{:S(2)}) copy-start(f32[32,256]{1,0:T(8,128)S(1)} %sub.13) | copy-start | bytes 98308
  133.3 12.9 %slice-start = ((s8[8388608]{0:T(1024)(128)(4,1)}), s8[4194304]{0:T(1024)(128)(4,1)S(1)}, s32[]{:S(2)}) async-start(s8[8388608]{0:T(1024)(128)(4,1)} %bitcast.118), calls=%async_computation.5 | async-start | bytes 8388608
  133.3 12.9 %slice-start.1 = ((s8[8388608]{0:T(1024)(128)(4,1)}), s8[4194304]{0:T(1024)(128)(4,1)S(1)}, s32[]{:S(2)}) async-start(s8[8388608]{0:T(1024)(128)(4,1)} %bitcast.118), calls=%async_computation.6 | async-start | bytes 8388608
  157.1 274.6 %all-reduce.7.cloned.1.call-start = ((), (), s32[]{:S(2)}) async-start(), calls=%async_computation.1 | async-start | bytes 1835008 | tf_op jit(solution)/shard_map/psum | solution.py:91
  318.9 112.7 %copy-start.1 = (f32[14,128,128]{2,1,0:T(8,128)S(1)}, f32[14,128,128]{2,1,0:T(8,128)}, u32[]{:S(2)}) copy-start(f32[14,128,128]{2,1,0:T(8,128)} %get-tuple-element.9) | copy-start | bytes 2752516
  318.9 112.7 %copy-start.2 = (f32[14,128,128]{2,1,0:T(8,128)S(1)}, f32[14,128,128]{2,1,0:T(8,128)}, u32[]{:S(2)}) copy-start(f32[14,128,128]{2,1,0:T(8,128)} %get-tuple-element.10) | copy-start | bytes 2752516
  335.2 328.9 %all-reduce.9.cloned.1.call-start = ((), (), s32[]{:S(2)}) async-start(), calls=%async_computation.2 | async-start | bytes 1835008 | tf_op jit(solution)/shard_map/psum | solution.py:91
  568.1 329.9 %all-reduce.11.cloned.1.call-start = ((), (), s32[]{:S(2)}) async-start(), calls=%async_computation.3 | async-start | bytes 1835008 | tf_op jit(solution)/shard_map/psum | solution.py:91
  724.7 0.9 copy-start.4
Sparse Core Ops, SparseCore 0:
  25.8 42.7 all-gather.1
  157.2 100.9 all-reduce.12
  335.3 96.2 all-reduce.6
  568.3 95.8 all-reduce.8
  802.2 95.8 all-reduce.10
where the time goes:
time: 944 us; the launch traced here: 938 us
  waiting for transfers between devices  432 us (46%)
  blocking collectives  304 us (32%)
  matrix products  127 us (13%)
  other arithmetic  36.9 us (4%)
  between operations  21.2 us (2%)
  local copies, waits for them, and re-layouts  17.1 us (2%)
    psum x3, waiting for transfers between devices, local(): reduced = lax.psum(curvature_partial_value, 'view')  288 us
    psum x3, blocking collectives, local(): curvature_pixel_vec = lax.psum(partial_value, 'scene')  131 us
    psum x5, blocking collectives, inner_sum(): return lax.psum(local_sum, 'scene')  129 us
    psum x1, waiting for transfers between devices, local(): gradient, curv_diag = lax.psum((grad_part, diag_part), 'view')  101 us
    psum x1, blocking collectives, local(): render = lax.psum(render_part, 'scene')  43.5 us
    all_gather x1, waiting for transfers between devices, local(): all_logs = lax.all_gather(block_log, 'scene', axis=1, tiled=True)  42.5 us
    dot_general x4, matrix products, transpose_apply(): jnp.einsum('tcq,tjqg->ctjg', pixel_basis, slope_now * spread, precision=h...  40 us
    dot_general x3, matrix products, local(): jnp.einsum('tcq,ctjg->tjqg', pixel_basis, forward_pieces[:param_count - 1...  36.4 us
  transfers between devices with their start and end apart: 5, of which 5 were waited for; matrix products, arithmetic and copies ran while one was open for 0% of the time, Pallas kernels for 0%

commit v1 on v0

--- a/solution.py
+++ b/solution.py
@@ -86,7 +86,11 @@
             slopes * projected + weight * forward_pieces[param_count - 1][:, :, None, :],
             axis=(1, 3),
         )
-        curvature_pixel_vec = lax.psum(partial_value, "scene")
+        curvature_pixel_vec = partial_value
+        for hop in (1, 2, 4, 8):
+            curvature_pixel_vec = curvature_pixel_vec + lax.ppermute(
+                curvature_pixel_vec, "scene", [(dev, dev ^ hop) for dev in range(16)]
+            )
         curvature_partial_value = transpose_apply(weight, slopes, curvature_pixel_vec)
         reduced = lax.psum(curvature_partial_value, "view")
         image_dir = reduced + (damping * curv_diag + ridge_term) * direction

time: 944 us -> 852 us (0.903)
  blocking collectives: 304 us -> 172 us
  waiting for transfers between devices: 432 us -> 457 us
  starting transfers between devices: 0.42 us -> 23.8 us
  other arithmetic: 36.9 us -> 27.1 us
    psum x3 -> x0, blocking collectives: 131 us -> none  [local(): curvature_pixel_vec = lax.psum(partial_value, 'scene')]
    ppermute x0 -> x12, waiting for transfers between devices: none -> 24 us  [local(): lax.ppermute(curvature_pixel_vec, 'scene', [(dev, dev ^ hop) for dev in r...]
    ppermute x0 -> x12, starting transfers between devices: none -> 23.3 us  [local(): lax.ppermute(curvature_pixel_vec, 'scene', [(dev, dev ^ hop) for dev in r...]
    reduce_sum x4, other arithmetic: 16.1 us -> 6.11 us  [transpose_apply(): colour_term = jnp.sum(weight_now * spread, axis=2)]
  transfers between devices with their start and end apart: 5 -> 17, of which waited for: 5 -> 17; matrix products, arithmetic and copies ran while one was open for 0% -> 0% of each run, Pallas kernels for 0% -> 0%
where the time goes in v1:
time: 852 us; the launch traced here: 845 us
  waiting for transfers between devices  457 us (54%)
  blocking collectives  172 us (20%)
  matrix products  126 us (15%)
  other arithmetic  27.1 us (3%)
  starting transfers between devices  23.8 us (3%)
  between operations  21.2 us (2%)
  local copies, waits for them, and re-layouts  17.2 us (2%)
    psum x3, waiting for transfers between devices, local(): reduced = lax.psum(curvature_partial_value, 'view')  290 us
    psum x5, blocking collectives, inner_sum(): return lax.psum(local_sum, 'scene')  129 us
    psum x1, waiting for transfers between devices, local(): gradient, curv_diag = lax.psum((grad_part, diag_part), 'view')  101 us
    psum x1, blocking collectives, local(): render = lax.psum(render_part, 'scene')  43.5 us
    all_gather x1, waiting for transfers between devices, local(): all_logs = lax.all_gather(block_log, 'scene', axis=1, tiled=True)  42.4 us
    dot_general x3, matrix products, local(): jnp.einsum('tcq,ctjg->tjqg', pixel_basis, forward_pieces[:param_count - 1...  40.3 us
    dot_general x4, matrix products, transpose_apply(): jnp.einsum('tcq,tjqg->ctjg', pixel_basis, slope_now * spread, precision=h...  35.5 us
    ppermute x12, waiting for transfers between devices, local(): lax.ppermute(curvature_pixel_vec, 'scene', [(dev, dev ^ hop) for dev in r...  24 us
  transfers between devices with their start and end apart: 17, of which 17 were waited for; matrix products, arithmetic and copies ran while one was open for 0% of the time, Pallas kernels for 0%

profile of v1, /device:TPU:1, one launch (start us, length us, event | category | flops | bytes accessed | tf_op | source)
XLA Modules:
  0.0 845.4 jit_solution(5751626245685515046)
XLA Ops:
  11.0 14.0 %fusion.19 = (f32[32,2,256]{2,1,0:T(2,128)S(1)}, f32[32,2,128,256]{3,2,1,0:T(8,128)}) fusion(f32[13,32,2,128]{3,0,2,1:T(8,128)S(1)} %bitcast.150, f32[32,13,256,1]{2,0,1,3:T(8,128)} %bitcast.130), kind=kOutput, calls=%fused_computation.35 | convolution fusion | flops 339722240 | bytes 9306112 | tf_op jit(solution)/shard_map/tcq,ctjg->tjqg/dot_general | solution.py:29
  26.2 42.4 %all-gather.2.cloned.1.call-done = f32[32,32,256]{2,0,1:T(8,128)} async-done(((f32[32,2,256]{2,0,1:T(8,128)}), f32[32,32,256]{2,0,1:T(8,128)}) %all-gather.2.cloned.1.call-update) | async-done | bytes 1048592 | tf_op jit(solution)/shard_map/all_gather | solution.py:35
  70.8 18.9 %bitcast_multiply_fusion.3 = (f32[32,2,256,128]{2,3,1,0:T(8,128)}, f32[32,256]{1,0:T(8,128)S(1)}, f32[32,2,256,128]{2,3,1,0:T(8,128)}) fusion(f32[32,2,128,256]{3,2,1,0:T(8,128)} %get-tuple-element.14, f32[32,2,128]{2,1,0:T(2,128)S(1)} %bitcast.156, f32[32,2,256]{2,1,0:T(2,128)S(1)} %fusion.27), kind=kOutput, calls=%fused_computation.13 | convolution fusion | flops 3240108032 | bytes 25296896 | tf_op jit(solution)/shard_map/tjqg,gh->tjqh/dot_general | solution.py:32
  89.7 43.5 %psum.84 = f32[32,256]{1,0:T(8,128)S(1)} all-reduce(f32[32,256]{1,0:T(8,128)S(1)} %get-tuple-element.12), channel_id=1, replica_groups=mesh['view'=16,'scene'=16] {'scene'}, use_global_device_ids=true, to_apply=%region_2.4 | all-reduce | flops 8192 | bytes 65536 | tf_op jit(solution)/shard_map/psum | solution.py:46
  133.3 10.5 %fusion.15 = f32[32,2,128,13]{2,3,1,0:T(8,128)S(1)} fusion(f32[32,2,256,128]{2,3,1,0:T(8,128)} %get-tuple-element.11, f32[32,256]{1,0:T(8,128)S(1)} %sub.13, f32[32,13,256,1]{2,0,1,3:T(8,128)S(1)} %bitcast.131), kind=kOutput, calls=%fused_computation.30 | convolution fusion | flops 329252864 | bytes 9273344 | tf_op jit(solution)/shard_map/tcq,tjqg->ctjg/dot_general | solution.py:56
  146.4 7.5 fusion.13
  157.3 101.0 %all-reduce.13.cloned.1.call-done = (f32[14,128,128]{2,1,0:T(8,128)}, f32[14,128,128]{2,1,0:T(8,128)}) async-done(((f32[14,128,128]{2,1,0:T(8,128)}, f32[14,128,128]{2,1,0:T(8,128)}), (f32[14,128,128]{2,1,0:T(8,128)}, f32[14,128,128]{2,1,0:T(8,128)})) %all-reduce.13.cloned.1.call-update) | async-done | bytes 1835024 | tf_op jit(solution)/shard_map/psum | solution.py:65
  261.3 12.5 %fusion.5 = f32[32,256]{1,0:T(8,128)S(1)} fusion(f32[32,2,256,128]{2,3,1,0:T(8,128)} %get-tuple-element.11, f32[32,2,256,128]{2,3,1,0:T(8,128)} %get-tuple-element.15, f32[32,2,128]{2,1,0:T(2,128)S(1)} %bitcast.157, f32[13,32,2,128]{3,0,2,1:T(8,128)S(1)} %bitcast.141, f32[32,13,256,1]{2,0,1,3:T(8,128)S(1)} %bitcast.132), kind=kOutput, calls=%fused_computation.12 | convolution fusion | flops 335536128 | bytes 17694720 | tf_op jit(solution)/shard_map/tcq,ctjg->tjqg/dot_general | solution.py:82
  283.5 6.0 collective-permute-start.3
  290.9 7.6 fusion.11
  301.6 97.6 %all-reduce.7.cloned.1.call-done = f32[14,128,128]{2,1,0:T(8,128)} async-done(((f32[14,128,128]{2,1,0:T(8,128)}), f32[14,128,128]{2,1,0:T(8,128)}) %all-reduce.7.cloned.1.call-update) | async-done | bytes 917520 | tf_op jit(solution)/shard_map/psum | solution.py:95
  401.4 26.2 %all-reduce = (f32[]{:T(128)}, f32[]{:T(128)}) all-reduce(f32[]{:T(128)} %get-tuple-element.6, f32[]{:T(128)} %get-tuple-element.5), channel_id=1, replica_groups=mesh['view'=16,'scene'=16] {'scene'}, use_global_device_ids=true, to_apply=%region_8.10 | all-reduce | flops 2 | bytes 16 | tf_op jit(solution)/shard_map/psum | solution.py:69
  431.3 25.2 %psum.90 = f32[]{:T(128)} all-reduce(f32[]{:T(128)} %multiply_reduce_fusion.9), channel_id=1, replica_groups=mesh['view'=16,'scene'=16] {'scene'}, use_global_device_ids=true, to_apply=%region_15.17 | all-reduce | flops 1 | bytes 8 | tf_op jit(solution)/shard_map/psum | solution.py:69
  464.9 13.9 %fusion.3 = f32[32,256]{1,0:T(8,128)S(1)} fusion(f32[32,2,256,128]{2,3,1,0:T(8,128)} %get-tuple-element.11, f32[32,2,256,128]{2,3,1,0:T(8,128)} %get-tuple-element.15, f32[32,2,128]{2,1,0:T(2,128)S(1)} %bitcast.158, f32[13,32,2,128]{3,0,2,1:T(8,128)S(1)} %bitcast.142, f32[32,13,256,1]{2,0,1,3:T(8,128)S(1)} %bitcast.134), kind=kOutput, calls=%fused_computation.9 | convolution fusion | flops 335536128 | bytes 17694720 | tf_op jit(solution)/shard_map/tcq,ctjg->tjqg/dot_general | solution.py:82
  486.9 4.7 collective-permute-start.7
  494.1 7.6 fusion.9
  504.7 96.2 %all-reduce.9.cloned.1.call-done = f32[14,128,128]{2,1,0:T(8,128)} async-done(((f32[14,128,128]{2,1,0:T(8,128)}), f32[14,128,128]{2,1,0:T(8,128)}) %all-reduce.9.cloned.1.call-update) | async-done | bytes 917520 | tf_op jit(solution)/shard_map/psum | solution.py:95
  602.9 26.2 %psum.92 = f32[]{:T(128)} all-reduce(f32[]{:T(128)} %multiply_reduce_fusion.8), channel_id=1, replica_groups=mesh['view'=16,'scene'=16] {'scene'}, use_global_device_ids=true, to_apply=%region_20.22 | all-reduce | flops 1 | bytes 8 | tf_op jit(solution)/shard_map/psum | solution.py:69
  632.9 25.2 %psum.93 = f32[]{:T(128)} all-reduce(f32[]{:T(128)} %multiply_reduce_fusion.7), channel_id=1, replica_groups=mesh['view'=16,'scene'=16] {'scene'}, use_global_device_ids=true, to_apply=%region_22.24 | all-reduce | flops 1 | bytes 8 | tf_op jit(solution)/shard_map/psum | solution.py:69
  667.7 13.9 %fusion.1 = f32[32,256]{1,0:T(8,128)S(1)} fusion(f32[32,2,256,128]{2,3,1,0:T(8,128)} %get-tuple-element.11, f32[32,2,256,128]{2,3,1,0:T(8,128)} %get-tuple-element.15, f32[32,2,128]{2,1,0:T(2,128)S(1)} %bitcast.159, f32[13,32,2,128]{3,0,2,1:T(8,128)S(1)} %bitcast.140, f32[32,13,256,1]{2,0,1,3:T(8,128)S(1)} %bitcast.136), kind=kOutput, calls=%fused_computation.6 | convolution fusion | flops 335536128 | bytes 17694720 | tf_op jit(solution)/shard_map/tcq,ctjg->tjqg/dot_general | solution.py:82
  689.7 4.4 collective-permute-start.11
  696.6 9.8 %fusion.7 = f32[32,2,128,13]{2,3,1,0:T(8,128)S(1)} fusion(f32[32,2,256,128]{2,3,1,0:T(8,128)} %get-tuple-element.11, f32[32,256]{1,0:T(8,128)S(1)} %add.144, f32[32,13,256,1]{2,0,1,3:T(8,128)S(1)} %bitcast.137), kind=kOutput, calls=%fused_computation.18 | convolution fusion | flops 329252864 | bytes 9273344 | tf_op jit(solution)/shard_map/tcq,tjqg->ctjg/dot_general | solution.py:56
  709.4 96.2 %all-reduce.11.cloned.1.call-done = f32[14,128,128]{2,1,0:T(8,128)} async-done(((f32[14,128,128]{2,1,0:T(8,128)}), f32[14,128,128]{2,1,0:T(8,128)}) %all-reduce.11.cloned.1.call-update) | async-done | bytes 917520 | tf_op jit(solution)/shard_map/psum | solution.py:95
  807.9 26.2 %psum.95 = f32[]{:T(128)} all-reduce(f32[]{:T(128)} %multiply_reduce_fusion.6), channel_id=1, replica_groups=mesh['view'=16,'scene'=16] {'scene'}, use_global_device_ids=true, to_apply=%region_27.29 | all-reduce | flops 1 | bytes 8 | tf_op jit(solution)/shard_map/psum | solution.py:69
  (142 shorter events, 87.0 us)
Async XLA Ops:
  7.2 61.4 %all-gather.2.cloned.1.call-start = ((), (), s32[]{:S(2)}) async-start(), calls=%async_computation | async-start | bytes 1114112 | tf_op jit(solution)/shard_map/all_gather | solution.py:35
  25.7 232.6 %all-reduce.13.cloned.1.call-start = ((), (), s32[]{:S(2)}) async-start(), calls=%async_computation.4 | async-start | bytes 3670016 | tf_op jit(solution)/shard_map/psum | solution.py:65
  70.8 62.5 %copy-start.7 = (f32[32,256]{1,0:T(8,128)S(1)}, f32[32,256]{1,0:T(8,128)}, u32[]{:S(2)}) copy-start(f32[32,256]{1,0:T(8,128)} %param.11) | copy-start | bytes 98308
  157.2 242.0 %all-reduce.7.cloned.1.call-start = ((), (), s32[]{:S(2)}) async-start(), calls=%async_computation.1 | async-start | bytes 1835008 | tf_op jit(solution)/shard_map/psum | solution.py:95
  261.3 37.2 %slice-start.6 = ((s8[8388608]{0:T(1024)(128)(4,1)}), s8[4194304]{0:T(1024)(128)(4,1)S(1)}, s32[]{:S(2)}) async-start(s8[8388608]{0:T(1024)(128)(4,1)} %bitcast.124), calls=%async_computation.11 | async-start | bytes 8388608
  261.3 37.2 %slice-start.7 = ((s8[8388608]{0:T(1024)(128)(4,1)}), s8[4194304]{0:T(1024)(128)(4,1)S(1)}, s32[]{:S(2)}) async-start(s8[8388608]{0:T(1024)(128)(4,1)} %bitcast.124), calls=%async_computation.12 | async-start | bytes 8388608
  273.8 3.2 collective-permute-start
  277.1 2.8 collective-permute-start.1
  279.8 3.7 collective-permute-start.2
  283.5 7.4 collective-permute-start.3
  290.9 108.3 %copy-start.1 = (f32[14,128,128]{2,1,0:T(8,128)S(1)}, f32[14,128,128]{2,1,0:T(8,128)}, u32[]{:S(2)}) copy-start(f32[14,128,128]{2,1,0:T(8,128)} %get-tuple-element.9) | copy-start | bytes 2752516
  290.9 108.2 %copy-start.2 = (f32[14,128,128]{2,1,0:T(8,128)S(1)}, f32[14,128,128]{2,1,0:T(8,128)}, u32[]{:S(2)}) copy-start(f32[14,128,128]{2,1,0:T(8,128)} %get-tuple-element.10) | copy-start | bytes 2752516
  301.5 299.3 %all-reduce.9.cloned.1.call-start = ((), (), s32[]{:S(2)}) async-start(), calls=%async_computation.2 | async-start | bytes 1835008 | tf_op jit(solution)/shard_map/psum | solution.py:95
  478.8 1.6 collective-permute-start.4
  480.4 2.8 collective-permute-start.5
  483.2 3.7 collective-permute-start.6
  486.9 7.1 collective-permute-start.7
  504.6 301.0 %all-reduce.11.cloned.1.call-start = ((), (), s32[]{:S(2)}) async-start(), calls=%async_computation.3 | async-start | bytes 1835008 | tf_op jit(solution)/shard_map/psum | solution.py:95
  667.7 38.8 %slice-start.10 = ((s8[8388608]{0:T(1024)(128)(4,1)}), s8[4194304]{0:T(1024)(128)(4,1)S(1)}, s32[]{:S(2)}) async-start(s8[8388608]{0:T(1024)(128)(4,1)} %bitcast.128), calls=%async_computation.15 | async-start | bytes 8388608
  667.7 38.8 %slice-start.11 = ((s8[8388608]{0:T(1024)(128)(4,1)}), s8[4194304]{0:T(1024)(128)(4,1)S(1)}, s32[]{:S(2)}) async-start(s8[8388608]{0:T(1024)(128)(4,1)} %bitcast.128), calls=%async_computation.16 | async-start | bytes 8388608
  681.6 1.6 collective-permute-start.8
  683.2 2.8 collective-permute-start.9
  686.0 3.7 collective-permute-start.10
  689.7 6.9 collective-permute-start.11
  (13 other events, 273.9 us)
Sparse Core Ops, SparseCore 0:
  25.8 42.7 all-gather.1
  157.3 100.9 all-reduce.12
  301.6 97.4 all-reduce.6
  504.8 96.0 all-reduce.8
  709.6 95.9 all-reduce.10
